TPU v7x, 256 devices: a whole 4x4x8 slice. The times are simulated.
256 devices in a mesh: src: 32 (over z, x), tgt: 8 (over y, core).
Axes of the slice: x: 4, y: 4, z: 8, core: 2. Of those that a mesh axis runs over, the one named last changes fastest.
Arguments:
- src_embed: float32 [65536, 256], P(('src', 'tgt')), may hold values from -7.5 to 7.5
- tgt_embed: float32 [32768, 256], P(('tgt', 'src')), may hold values from -7.5 to 7.5
- log_src: float32 [65536], P('src'), may hold values from -1.25 to 2.35
- log_tgt: float32 [32768], P('tgt'), may hold values from -1.25 to 2.35
- tgt_pot: float32 [32768], P('tgt'), may hold values from -1 to 6
Outputs:
- src_dual: float32 [65536], P('src')
- tgt_dual: float32 [32768], P('tgt')
All inputs are finite; a program needn't handle non-finite values.
Results may differ from a plain program's by a relative error of at most 0.0003.
Values sent between devices are 32-bit elements; how exact they have to be, the bound alone decides.
No kernel may reach another device: no remote copies, remote signals or barrier semaphores. Data moves between devices by JAX's collectives and lax.ppermute only.
A program may use at most 128 MiB of HBM per device.

v0:
```python
import jax
import jax.numpy as jnp
from jax import lax
from jax.sharding import PartitionSpec as P

EPSILON = 0.05


def cross_inner(left, right):
    return lax.dot_general(
        left,
        right,
        (((1,), (1,)), ((), ())),
        precision=lax.Precision.HIGHEST,
        preferred_element_type=jnp.float32,
    )


def row_lse(scores):
    highest = lax.pmax(jnp.max(scores, axis=1), "tgt")
    totals = lax.psum(jnp.sum(jnp.exp(scores - highest[:, None]), axis=1), "tgt")
    return highest + jnp.log(totals)


def column_lse(scores):
    highest = lax.pmax(jnp.max(scores, axis=0), "src")
    totals = lax.psum(jnp.sum(jnp.exp(scores - highest[None, :]), axis=0), "src")
    return highest + jnp.log(totals)


def shards(src_embed, tgt_embed, log_src, log_tgt, tgt_pot):
    width = src_embed.shape[1]
    targets = lax.all_gather(tgt_embed, "src", axis=0, tiled=True)
    tgt_norm = jnp.sum(targets * targets, axis=1)
    piece = lax.all_gather(src_embed, "tgt", axis=0, tiled=True)
    src_norm = jnp.sum(piece * piece, axis=1)
    cost = (src_norm[:, None] + tgt_norm[None, :] - 2.0 * cross_inner(piece, targets)) / width
    tgt_dual = tgt_pot
    src_dual = -EPSILON * row_lse(log_tgt[None, :] + (tgt_dual[None, :] - cost) / EPSILON)
    tgt_dual = -EPSILON * column_lse(log_src[:, None] + (src_dual[:, None] - cost) / EPSILON)
    return (src_dual, tgt_dual)


def solution(mesh):
    in_specs = (P(("src", "tgt"), None), P(("tgt", "src"), None), P("src"), P("tgt"), P("tgt"))
    out_specs = (P("src"), P("tgt"))
    return jax.shard_map(shards, mesh=mesh, in_specs=in_specs, out_specs=out_specs, check_vma=False)
```

profile of v0, /device:TPU:0, one launch (start us, length us, event | category | flops | bytes accessed | tf_op | source)
XLA Modules:
  0.0 522.3 jit_solution(12428725631582622613)
XLA Ops:
  7.2 0.0 all-gather.3.cloned.1.call-start
  7.2 0.7 all-gather.3.cloned.1.call-update
  7.9 0.0 all-gather.5.cloned.1.call-start
  7.9 0.7 all-gather.5.cloned.1.call-update
  8.6 30.4 %all-gather.3.cloned.1.call-done = f32[2048,256]{1,0:T(8,128)} async-done(((f32[256,256]{1,0:T(8,128)}), f32[2048,256]{1,0:T(8,128)}) %all-gather.3.cloned.1.call-update) | async-done | bytes 2097168 | tf_op jit(solution)/shard_map/all_gather | solution.py:35
  39.0 1.9 multiply_reduce_fusion.1
  40.9 82.8 %all-gather.5.cloned.1.call-done = f32[4096,256]{1,0:T(8,128)} async-done(((f32[128,256]{1,0:T(8,128)}), f32[4096,256]{1,0:T(8,128)}) %all-gather.5.cloned.1.call-update) | async-done | bytes 4194320 | tf_op jit(solution)/shard_map/all_gather | solution.py:33
  123.8 2.8 multiply_reduce_fusion
  126.6 0.0 copy-start.2
  126.6 0.0 copy-start.3
  126.6 41.2 %fusion = (f32[2048]{0:T(1024)S(1)}, f32[2048,4096]{1,0:T(8,128)}) fusion(f32[4096]{0:T(1024)} %param.9, f32[4096]{0:T(1024)} %param.8, f32[2048,256]{1,0:T(8,128)} %all-gather.3.cloned.1.call-done, f32[4096,256]{1,0:T(8,128)} %all-gather.5.cloned.1.call-done, f32[4096]{0:T(1024)S(1)} %multiply_reduce_fusion, f32[2048]{0:T(1024)S(1)} %multiply_reduce_fusion.1), kind=kOutput, calls=%fused_computation.5 | convolution fusion | flops 25836910592 | bytes 39911424 | tf_op jit(solution)/shard_map/dot_general | solution.py:10
  167.8 0.0 copy-start.1
  167.8 12.8 %pmax.14 = f32[2048]{0:T(1024)S(1)} all-reduce(f32[2048]{0:T(1024)S(1)} %get-tuple-element.2), channel_id=1, replica_groups=mesh['src'=32,'tgt'=8] {'tgt'}, use_global_device_ids=true, to_apply=%region_3.0 | all-reduce | flops 2048 | bytes 16384 | tf_op jit(solution)/shard_map/pmax | solution.py:20
  180.6 0.0 copy-done.2
  180.6 0.0 copy-done.3
  180.7 15.2 %exponential_reduce_fusion.1 = f32[2048]{0:T(1024)S(1)} fusion(f32[2048,4096]{1,0:T(8,128)} %get-tuple-element.3, f32[2048]{0:T(1024)S(1)} %pmax.14, f32[4096]{0:T(1024)S(1)} %copy-done.2, f32[4096]{0:T(1024)S(1)} %copy-done.3), kind=kLoop, calls=%fused_computation.2 | loop fusion | flops 41940992 | bytes 33603584 | tf_op jit(solution)/shard_map/reduce_sum | solution.py:21
  195.8 12.7 %psum.14 = f32[2048]{0:T(1024)S(1)} all-reduce(f32[2048]{0:T(1024)S(1)} %exponential_reduce_fusion.1), channel_id=1, replica_groups=mesh['src'=32,'tgt'=8] {'tgt'}, use_global_device_ids=true, to_apply=%region_5.0 | all-reduce | flops 2048 | bytes 16384 | tf_op jit(solution)/shard_map/psum | solution.py:21
  208.5 0.0 copy-done.1
  208.5 0.0 copy-start
  208.5 13.7 %fusion.1 = f32[4096]{0:T(1024)S(1)} fusion(f32[2048,4096]{1,0:T(8,128)} %get-tuple-element.3, f32[2048]{0:T(1024)S(1)} %add_multiply_fusion.1, f32[2048]{0:T(1024)S(1)} %copy-done.1), kind=kLoop, calls=%fused_computation.6 | loop fusion | flops 33550336 | bytes 33587200 | tf_op jit(solution)/shard_map/reduce_max | solution.py:26
  222.2 139.8 %pmax.15 = f32[4096]{0:T(1024)S(1)} all-reduce(f32[4096]{0:T(1024)S(1)} %fusion.1), channel_id=1, replica_groups=mesh['src'=32,'tgt'=8] {'src'}, use_global_device_ids=true, to_apply=%region_7.0 | all-reduce | flops 4096 | bytes 32768 | tf_op jit(solution)/shard_map/pmax | solution.py:26
  362.1 15.1 %exponential_reduce_fusion = f32[4096]{0:T(1024)S(1)} fusion(f32[2048,4096]{1,0:T(8,128)} %get-tuple-element.3, f32[4096]{0:T(1024)S(1)} %pmax.15, f32[2048]{0:T(1024)S(1)} %add_multiply_fusion.1, f32[2048]{0:T(1024)S(1)} %copy-done.1), kind=kLoop, calls=%fused_computation | loop fusion | flops 41938944 | bytes 33603584 | tf_op jit(solution)/shard_map/reduce_sum | solution.py:27
  377.2 0.0 copy-done
  377.2 137.7 %psum.15 = f32[4096]{0:T(1024)S(1)} all-reduce(f32[4096]{0:T(1024)S(1)} %exponential_reduce_fusion), channel_id=1, replica_groups=mesh['src'=32,'tgt'=8] {'src'}, use_global_device_ids=true, to_apply=%region_9.0 | all-reduce | flops 4096 | bytes 32768 | tf_op jit(solution)/shard_map/psum | solution.py:27
  514.9 0.6 add_multiply_fusion
  (1 shorter events, 0.0 us)
Async XLA Ops:
  7.2 31.8 %all-gather.3.cloned.1.call-start = ((), (), s32[]{:S(2)}) async-start(), calls=%async_computation | async-start | bytes 2359296 | tf_op jit(solution)/shard_map/all_gather | solution.py:35
  7.9 115.9 %all-gather.5.cloned.1.call-start = ((), (), s32[]{:S(2)}) async-start(), calls=%async_computation.1 | async-start | bytes 4325376 | tf_op jit(solution)/shard_map/all_gather | solution.py:33
  126.6 54.1 %copy-start.2 = (f32[4096]{0:T(1024)S(1)}, f32[4096]{0:T(1024)}, u32[]{:S(2)}) copy-start(f32[4096]{0:T(1024)} %param.9) | copy-start | bytes 49156
  126.6 54.1 %copy-start.3 = (f32[4096]{0:T(1024)S(1)}, f32[4096]{0:T(1024)}, u32[]{:S(2)}) copy-start(f32[4096]{0:T(1024)} %param.8) | copy-start | bytes 49156
  167.8 40.7 %copy-start.1 = (f32[2048]{0:T(1024)S(1)}, f32[2048]{0:T(1024)}, u32[]{:S(2)}) copy-start(f32[2048]{0:T(1024)} %param.7) | copy-start | bytes 24580
  208.5 168.7 %copy-start = (f32[2048]{0:T(1024)}, f32[2048]{0:T(1024)S(1)}, u32[]{:S(2)}) copy-start(f32[2048]{0:T(1024)S(1)} %add_multiply_fusion.1) | copy-start | bytes 24580
Sparse Core Ops, SparseCore 0:
  9.8 29.1 all-gather.2
  41.6 82.1 all-gather.4
where the time goes:
time: 523 us; the launch traced here: 522 us
  blocking collectives  303 us (58%)
  waiting for transfers between devices  115 us (22%)
  other arithmetic  49.3 us (9%)
  matrix products  41.2 us (8%)
  between operations  14.1 us (3%)
    pmax x1, blocking collectives, column_lse(): highest = lax.pmax(jnp.max(scores, axis=0), 'src')  140 us
    psum x1, blocking collectives, column_lse(): lax.psum(jnp.sum(jnp.exp(scores - highest[None, :]), axis=0), 'src')  138 us
    all_gather x1, waiting for transfers between devices, shards(): targets = lax.all_gather(tgt_embed, 'src', axis=0, tiled=True)  82.8 us
    dot_general x1, matrix products, cross_inner(): lax.dot_general(left, right, (((1,), (1,)), ((), ())), precision=lax.Prec...  41.2 us
    all_gather x1, waiting for transfers between devices, shards(): piece = lax.all_gather(src_embed, 'tgt', axis=0, tiled=True)  30.4 us
    reduce_sum x1, other arithmetic, row_lse(): jnp.sum(jnp.exp(scores - highest[:, None]), axis=1)  15.2 us
    reduce_sum x1, other arithmetic, column_lse(): jnp.sum(jnp.exp(scores - highest[None, :]), axis=0)  15.1 us
    reduce_max x1, other arithmetic, column_lse(): highest = lax.pmax(jnp.max(scores, axis=0), 'src')  13.7 us
  transfers between devices with their start and end apart: 2, of which 2 were waited for; matrix products, arithmetic and copies ran while one was open for 0% of the time, Pallas kernels for 0%

commit v1 on v0

--- a/solution.py
+++ b/solution.py
@@ -30,7 +30,10 @@
 
 def shards(src_embed, tgt_embed, log_src, log_tgt, tgt_pot):
     width = src_embed.shape[1]
-    targets = lax.all_gather(tgt_embed, "src", axis=0, tiled=True)
+    count = lax.axis_size("src")
+    shards_2 = jnp.stack([tgt_embed for _ in range(count)])
+    shards_2 = lax.all_to_all(shards_2, "src", split_axis=0, concat_axis=0)
+    targets = jnp.concatenate(shards_2, axis=0)
     tgt_norm = jnp.sum(targets * targets, axis=1)
     piece = lax.all_gather(src_embed, "tgt", axis=0, tiled=True)
     src_norm = jnp.sum(piece * piece, axis=1)

time: 523 us -> 516 us (0.987)
  waiting for transfers between devices: 115 us -> 92.3 us
  starting transfers between devices: 0.08 us -> 9.78 us
    all_gather x1 -> x0, waiting for transfers between devices: 82.8 us -> none  [shards(): targets = lax.all_gather(tgt_embed, 'src', axis=0, tiled=True)]
    all_to_all x0 -> x1, waiting for transfers between devices: none -> 60.4 us  [shards(): shards_2 = lax.all_to_all(shards_2, 'src', split_axis=0, concat_axis=0)]
    all_to_all x0 -> x1, starting transfers between devices: none -> 9.74 us  [shards(): shards_2 = lax.all_to_all(shards_2, 'src', split_axis=0, concat_axis=0)]
where the time goes in v1:
time: 516 us; the launch traced here: 515 us
  blocking collectives  305 us (59%)
  waiting for transfers between devices  92.3 us (18%)
  other arithmetic  49.3 us (10%)
  matrix products  41.2 us (8%)
  between operations  14.1 us (3%)
  starting transfers between devices  9.78 us (2%)
    pmax x1, blocking collectives, column_lse(): highest = lax.pmax(jnp.max(scores, axis=0), 'src')  141 us
    psum x1, blocking collectives, column_lse(): lax.psum(jnp.sum(jnp.exp(scores - highest[None, :]), axis=0), 'src')  138 us
    all_to_all x1, waiting for transfers between devices, shards(): shards_2 = lax.all_to_all(shards_2, 'src', split_axis=0, concat_axis=0)  60.4 us
    dot_general x1, matrix products, cross_inner(): lax.dot_general(left, right, (((1,), (1,)), ((), ())), precision=lax.Prec...  41.2 us
    all_gather x1, waiting for transfers between devices, shards(): piece = lax.all_gather(src_embed, 'tgt', axis=0, tiled=True)  31.2 us
    reduce_sum x1, other arithmetic, row_lse(): jnp.sum(jnp.exp(scores - highest[:, None]), axis=1)  15.2 us
    reduce_sum x1, other arithmetic, column_lse(): jnp.sum(jnp.exp(scores - highest[None, :]), axis=0)  15.1 us
    pmax x1, blocking collectives, row_lse(): highest = lax.pmax(jnp.max(scores, axis=1), 'tgt')  13.8 us
  transfers between devices with their start and end apart: 2, of which 2 were waited for; matrix products, arithmetic and copies ran while one was open for 0% of the time, Pallas kernels for 0%

profile of v1, /device:TPU:0, one launch (start us, length us, event | category | flops | bytes accessed | tf_op | source)
XLA Modules:
  0.0 514.9 jit_solution(18314471034097444825)
XLA Ops:
  7.2 3.3 stack.2
  10.5 9.7 %all-to-all-start = ((f32[32,128,256]{2,1,0:T(8,128)}), f32[32,128,256]{2,1,0:T(8,128)}, u32[]{:S(2)}, u32[]{:S(2)}) async-start(f32[32,128,256]{2,1,0:T(8,128)} %stack.2), calls=%async_computation | async-start | bytes 8388608 | tf_op jit(solution)/shard_map/all_to_all | solution.py:35
  20.2 0.0 all-gather.2.cloned.1.call-start
  20.3 0.7 all-gather.2.cloned.1.call-update
  20.9 31.2 %all-gather.2.cloned.1.call-done = f32[2048,256]{1,0:T(8,128)} async-done(((f32[256,256]{1,0:T(8,128)}), f32[2048,256]{1,0:T(8,128)}) %all-gather.2.cloned.1.call-update) | async-done | bytes 2097168 | tf_op jit(solution)/shard_map/all_gather | solution.py:38
  52.1 1.9 multiply_reduce_fusion.1
  54.1 60.4 %all-to-all-done = f32[32,128,256]{2,1,0:T(8,128)} async-done(((f32[32,128,256]{2,1,0:T(8,128)}), f32[32,128,256]{2,1,0:T(8,128)}, u32[]{:S(2)}, u32[]{:S(2)}) %all-to-all-start) | async-done | bytes 4194336 | tf_op jit(solution)/shard_map/all_to_all | solution.py:35
  114.5 2.8 multiply_reduce_fusion
  117.3 0.0 copy-start.2
  117.3 0.0 copy-start.3
  117.3 41.2 %fusion = (f32[2048]{0:T(1024)S(1)}, f32[2048,4096]{1,0:T(8,128)}) fusion(f32[4096]{0:T(1024)} %param.9, f32[4096]{0:T(1024)} %param.8, f32[2048,256]{1,0:T(8,128)} %all-gather.2.cloned.1.call-done, f32[4096,256]{1,0:T(8,128)} %bitcast.1, f32[4096]{0:T(1024)S(1)} %bitcast.4, f32[2048]{0:T(1024)S(1)} %multiply_reduce_fusion.1), kind=kOutput, calls=%fused_computation.5 | convolution fusion | flops 25836910592 | bytes 39911424 | tf_op jit(solution)/shard_map/dot_general | solution.py:10
  158.5 0.0 copy-start.1
  158.5 13.8 %pmax.14 = f32[2048]{0:T(1024)S(1)} all-reduce(f32[2048]{0:T(1024)S(1)} %get-tuple-element.2), channel_id=1, replica_groups=mesh['src'=32,'tgt'=8] {'tgt'}, use_global_device_ids=true, to_apply=%region_3.0 | all-reduce | flops 2048 | bytes 16384 | tf_op jit(solution)/shard_map/pmax | solution.py:20
  172.3 0.0 copy-done.2
  172.3 0.0 copy-done.3
  172.3 15.2 %exponential_reduce_fusion.1 = f32[2048]{0:T(1024)S(1)} fusion(f32[2048,4096]{1,0:T(8,128)} %get-tuple-element.3, f32[2048]{0:T(1024)S(1)} %pmax.14, f32[4096]{0:T(1024)S(1)} %copy-done.2, f32[4096]{0:T(1024)S(1)} %copy-done.3), kind=kLoop, calls=%fused_computation.2 | loop fusion | flops 41940992 | bytes 33603584 | tf_op jit(solution)/shard_map/reduce_sum | solution.py:21
  187.5 12.7 %psum.14 = f32[2048]{0:T(1024)S(1)} all-reduce(f32[2048]{0:T(1024)S(1)} %exponential_reduce_fusion.1), channel_id=1, replica_groups=mesh['src'=32,'tgt'=8] {'tgt'}, use_global_device_ids=true, to_apply=%region_5.0 | all-reduce | flops 2048 | bytes 16384 | tf_op jit(solution)/shard_map/psum | solution.py:21
  200.2 0.0 copy-done.1
  200.2 0.0 copy-start
  200.2 13.7 %fusion.1 = f32[4096]{0:T(1024)S(1)} fusion(f32[2048,4096]{1,0:T(8,128)} %get-tuple-element.3, f32[2048]{0:T(1024)S(1)} %add_multiply_fusion.1, f32[2048]{0:T(1024)S(1)} %copy-done.1), kind=kLoop, calls=%fused_computation.6 | loop fusion | flops 33550336 | bytes 33587200 | tf_op jit(solution)/shard_map/reduce_max | solution.py:26
  213.9 140.7 %pmax.15 = f32[4096]{0:T(1024)S(1)} all-reduce(f32[4096]{0:T(1024)S(1)} %fusion.1), channel_id=1, replica_groups=mesh['src'=32,'tgt'=8] {'src'}, use_global_device_ids=true, to_apply=%region_7.0 | all-reduce | flops 4096 | bytes 32768 | tf_op jit(solution)/shard_map/pmax | solution.py:26
  354.7 15.1 %exponential_reduce_fusion = f32[4096]{0:T(1024)S(1)} fusion(f32[2048,4096]{1,0:T(8,128)} %get-tuple-element.3, f32[4096]{0:T(1024)S(1)} %pmax.15, f32[2048]{0:T(1024)S(1)} %add_multiply_fusion.1, f32[2048]{0:T(1024)S(1)} %copy-done.1), kind=kLoop, calls=%fused_computation | loop fusion | flops 41938944 | bytes 33603584 | tf_op jit(solution)/shard_map/reduce_sum | solution.py:27
  369.8 0.0 copy-done
  369.8 137.7 %psum.15 = f32[4096]{0:T(1024)S(1)} all-reduce(f32[4096]{0:T(1024)S(1)} %exponential_reduce_fusion), channel_id=1, replica_groups=mesh['src'=32,'tgt'=8] {'src'}, use_global_device_ids=true, to_apply=%region_9.0 | all-reduce | flops 4096 | bytes 32768 | tf_op jit(solution)/shard_map/psum | solution.py:27
  507.4 0.6 add_multiply_fusion
  (1 shorter events, 0.0 us)
Async XLA Ops:
  10.5 104.0 %all-to-all-start = ((f32[32,128,256]{2,1,0:T(8,128)}), f32[32,128,256]{2,1,0:T(8,128)}, u32[]{:S(2)}, u32[]{:S(2)}) async-start(f32[32,128,256]{2,1,0:T(8,128)} %stack.2), calls=%async_computation | async-start | bytes 8388608 | tf_op jit(solution)/shard_map/all_to_all | solution.py:35
  20.2 31.9 %all-gather.2.cloned.1.call-start = ((), (), s32[]{:S(2)}) async-start(), calls=%async_computation.1 | async-start | bytes 2359296 | tf_op jit(solution)/shard_map/all_gather | solution.py:38
  117.3 55.0 %copy-start.2 = (f32[4096]{0:T(1024)S(1)}, f32[4096]{0:T(1024)}, u32[]{:S(2)}) copy-start(f32[4096]{0:T(1024)} %param.9) | copy-start | bytes 49156
  117.3 55.0 %copy-start.3 = (f32[4096]{0:T(1024)S(1)}, f32[4096]{0:T(1024)}, u32[]{:S(2)}) copy-start(f32[4096]{0:T(1024)} %param.8) | copy-start | bytes 49156
  158.5 41.7 %copy-start.1 = (f32[2048]{0:T(1024)S(1)}, f32[2048]{0:T(1024)}, u32[]{:S(2)}) copy-start(f32[2048]{0:T(1024)} %param.7) | copy-start | bytes 24580
  200.2 169.6 %copy-start = (f32[2048]{0:T(1024)}, f32[2048]{0:T(1024)S(1)}, u32[]{:S(2)}) copy-start(f32[2048]{0:T(1024)S(1)} %add_multiply_fusion.1) | copy-start | bytes 24580
Sparse Core Ops, SparseCore 0:
  22.9 29.2 all-gather.1
